TPU v7x, 256 devices: a whole 4x4x8 slice. The times are simulated.
256 devices in a mesh: seq: 32 (over y, z), head: 8 (over x, core).
Axes of the slice: x: 4, y: 4, z: 8, core: 2. Of those that a mesh axis runs over, the one named last changes fastest.
Arguments:
- inputs: bfloat16 [8192, 8192], P('seq'), may hold values from -6 to 6
- w_value: bfloat16 [8192, 4096], P('seq', 'head'), may hold values from -0.0625 to 0.0625
- log_decay: float32 [8192, 64], P('seq', 'head'), may hold values from -1 to 0
- b_proj: bfloat16 [8192, 128], P('seq'), may hold values from -0.5 to 0.5
- c_proj: bfloat16 [8192, 128], P('seq'), may hold values from -0.5 to 0.5
- grad_out: bfloat16 [8192, 4096], P('seq', 'head'), may hold values from -6 to 6
Outputs:
- grad_input: bfloat16 [8192, 8192], P('seq', 'head')
- grad_weight: float32 [8192, 4096], P('seq', 'head')
- grad_b: float32 [8192, 128], P('seq')
- grad_c: float32 [8192, 128], P('seq')
All inputs are finite; a program needn't handle non-finite values.
Results may differ from a plain program's by a relative error of at most 0.027.
Values may be sent and summed in bfloat16 or wider, within the bound.
A program may use at most 128 MiB of HBM per device.

v0:
```python
import jax
import jax.numpy as jnp
from jax import lax
from jax.sharding import PartitionSpec as P

SPAN = 256
HIGH = lax.Precision.HIGHEST


def carried_in(array, axis, combine, identity, reverse):
    length, index = (lax.axis_size(axis), lax.axis_index(axis))
    everything = jax.tree.map(
        lambda part, kind: lax.all_gather(part.astype(kind), axis),
        array,
        (jnp.bfloat16, jnp.bfloat16),
    )
    start = jax.tree.map(
        lambda part, zero: jnp.broadcast_to(jnp.asarray(zero, part.dtype), part.shape),
        array,
        identity,
    )

    def lap(k, before):
        at = length - 1 - k if reverse else k
        reached = at > index if reverse else at < index
        new = combine(
            before, jax.tree.map(lambda part, own: part[at].astype(own.dtype), everything, array)
        )
        return jax.tree.map(lambda a, b: jnp.where(reached, a, b), new, before)

    return lax.fori_loop(0, length, lap, start)


def link(earlier, later):
    return (earlier[0] * later[0], later[0][:, None, None] * earlier[1] + later[1])


def advance_once(carried, item):
    decay, local = item
    return (decay[:, None, None] * carried + local, carried)


def per_device(inputs, w_value, log_decay, b_proj, c_proj, grad_out):
    steps = inputs.shape[0]
    heads = log_decay.shape[1]
    columns = grad_out.shape[1]
    depth = columns // heads
    states = b_proj.shape[1]
    blocks = steps // SPAN
    w_full = lax.all_gather(w_value, "seq", axis=0, tiled=True)
    values = jnp.dot(inputs, w_full, preferred_element_type=jnp.float32).astype(jnp.bfloat16)
    xs = values.astype(jnp.float32).reshape(blocks, SPAN, heads, depth)
    dys = grad_out.astype(jnp.float32).reshape(blocks, SPAN, heads, depth)
    bs = b_proj.astype(jnp.float32).reshape(blocks, SPAN, states)
    cs = c_proj.astype(jnp.float32).reshape(blocks, SPAN, states)
    before_or_at = jnp.tril(jnp.ones((SPAN, SPAN), jnp.float32))
    cum_log = jnp.einsum(
        "tj,kjh->kth", before_or_at, log_decay.reshape(blocks, SPAN, heads), precision=HIGH
    )
    totals = cum_log[:, -1]
    grow = jnp.exp(cum_log)
    shrink = jnp.exp(totals[:, None] - cum_log)
    cum_heads = jnp.swapaxes(cum_log, 1, 2)
    rows = lax.broadcasted_iota(jnp.int32, (SPAN, SPAN), 0)
    cols = lax.broadcasted_iota(jnp.int32, (SPAN, SPAN), 1)
    lower = (rows >= cols)[None, None]
    diff = cum_heads[:, :, :, None] - cum_heads[:, :, None, :]
    decay_mat = jnp.exp(jnp.where(lower, diff, -jnp.inf))
    cross = jnp.einsum("kthp,kjhp->khtj", dys, xs, precision=HIGH)
    mixed = decay_mat * cross
    scores = jnp.einsum("ktn,kjn->ktj", cs, bs, precision=HIGH)
    span_decay = jnp.exp(totals)
    dev_decay = jnp.exp(jnp.sum(totals, axis=0))
    zero_state = jnp.zeros((heads, depth, states), jnp.float32)
    identity_matrix = (jnp.ones_like(dev_decay), zero_state)
    local_end = jnp.einsum("kjhp,kjh,kjn->khpn", xs, shrink, bs, precision=HIGH)
    dev_state, before = lax.scan(advance_once, zero_state, (span_decay, local_end))
    incoming = carried_in((dev_decay, dev_state), "seq", link, identity_matrix, False)[1]
    earlier = jnp.tril(jnp.ones((blocks, blocks), jnp.float32))
    through = jnp.einsum("kl,lh->kh", earlier, totals, precision=HIGH)
    lead = jnp.exp(through - totals)
    state_in = before + lead[:, :, None, None] * incoming[None]
    grad_c = jnp.einsum("kthp,khpn,kth->ktn", dys, state_in, grow, precision=HIGH)
    grad_c = grad_c + jnp.einsum("khtj,kjn->ktn", mixed, bs, precision=HIGH)
    local_back = jnp.einsum("kthp,kth,ktn->khpn", dys, grow, cs, precision=HIGH)
    dev_back, after = lax.scan(advance_once, zero_state, (span_decay, local_back), reverse=True)
    incoming_back = carried_in((dev_decay, dev_back), "seq", link, identity_matrix, True)[1]
    trail = jnp.exp(jnp.sum(totals, axis=0)[None] - through)
    grad_in = after + trail[:, :, None, None] * incoming_back[None]
    grad_vals = jnp.einsum("khst,kst,kshp->kthp", decay_mat, scores, dys, precision=HIGH)
    grad_vals = grad_vals + jnp.einsum("khpn,ktn,kth->kthp", grad_in, bs, shrink, precision=HIGH)
    grad_b = jnp.einsum("khst,ksn->ktn", mixed, cs, precision=HIGH)
    grad_b = grad_b + jnp.einsum("kthp,khpn,kth->ktn", xs, grad_in, shrink, precision=HIGH)
    grad_values = grad_vals.reshape(steps, columns).astype(jnp.bfloat16)
    grad_b, grad_c = (
        lax.psum(grad_b.reshape(steps, states).astype(jnp.bfloat16), "head").astype(jnp.float32),
        lax.psum(grad_c.reshape(steps, states).astype(jnp.bfloat16), "head").astype(jnp.float32),
    )
    term = lax.dot_general(
        grad_values, w_full, (((1,), (1,)), ((), ())), preferred_element_type=jnp.float32
    )
    grad_input = lax.psum_scatter(
        term.astype(jnp.bfloat16), "head", scatter_dimension=1, tiled=True
    )
    grad_weight = lax.psum_scatter(
        lax.dot_general(
            inputs, grad_values, (((0,), (0,)), ((), ())), preferred_element_type=jnp.float32
        ).astype(jnp.bfloat16),
        "seq",
        scatter_dimension=0,
        tiled=True,
    ).astype(jnp.float32)
    return (grad_input, grad_weight, grad_b, grad_c)


def solution(mesh):
    placed = (
        P("seq", None),
        P("seq", "head"),
        P("seq", "head"),
        P("seq", None),
        P("seq", None),
        P("seq", "head"),
    )
    return jax.shard_map(
        per_device,
        mesh=mesh,
        in_specs=placed,
        out_specs=(P("seq", "head"), P("seq", "head"), P("seq", None), P("seq", None)),
        check_vma=False,
    )
```

profile of v0, /device:TPU:8, one launch (start us, length us, event | category | flops | bytes accessed | tf_op | source)
XLA Modules:
  0.0 656.2 jit_solution(16976083974051187872)
XLA Ops:
  8.0 1.1 copy.24
  10.2 1.9 fusion.18
  12.4 41.5 %all-gather = bf16[32,1,8]{2,1,0:T(2,128)(2,1)S(1)} all-gather(bf16[1,1,8]{2,1,0:T(2,128)(2,1)S(1)} %copy.26), channel_id=2, replica_groups=mesh['seq'=32,'head'=8] {'seq'}, dimensions={0}, use_global_device_ids=true | all-gather | bytes 528 | tf_op jit(solution)/shard_map/all_gather | solution.py:13
  53.9 1.0 fusion.47
  55.0 55.8 %all-gather.7.cloned.1.call-done = bf16[8192,512]{1,0:T(8,128)(2,1)} async-done(((bf16[256,512]{1,0:T(8,128)(2,1)}), bf16[8192,512]{1,0:T(8,128)(2,1)}) %all-gather.7.cloned.1.call-update) | async-done | bytes 8388624 | tf_op jit(solution)/shard_map/all_gather | solution.py:50
  110.8 7.0 %convolution_convert_fusion.2 = bf16[256,512]{1,0:T(8,128)(2,1)S(1)} fusion(bf16[256,8192]{1,0:T(8,128)(2,1)} %param.10, bf16[8192,512]{1,0:T(8,128)(2,1)} %all-gather.7.cloned.1.call-done), kind=kOutput, calls=%fused_computation.21 | convolution fusion | flops 2147614720 | bytes 12845056 | tf_op jit(solution)/shard_map/dot_general | solution.py:51
  117.9 1.1 fusion.19
  119.0 73.8 %all-gather.9.cloned.1.call-done = bf16[256,64,128]{2,1,0:T(8,128)(2,1)} async-done(((bf16[8,64,128]{2,1,0:T(8,128)(2,1)}), bf16[256,64,128]{2,1,0:T(8,128)(2,1)}) %all-gather.9.cloned.1.call-update) | async-done | bytes 4194320 | tf_op jit(solution)/shard_map/all_gather | solution.py:13
  192.8 34.2 %while.40 = (s32[]{:T(128)}, f32[8,64,128]{2,1,0:T(8,128)S(1)}, s32[]{:T(128)}, bf16[32,8]{1,0:T(8,128)(2,1)S(1)}, bf16[32,8,64,128]{3,2,1,0:T(8,128)(2,1)}, /*index=5*/s32[]{:T(128)}, s32[]{:T(128)}, s32[]{:T(128)}, s32[]{:T(128)}) while((s32[]{:T(128)}, f32[8,64,128]{2,1,0:T(8,128)S(1)}, s32[]{:T(128)}, ...), condition=%wide.region_1.2_spmd.clone, body=%wide.region_0.1_spmd.clone.sunk | while | flops 327696 | bytes 655607 | solution.py:31
  193.9 1.0 fusion.66
  195.0 1.0 fusion.66
  196.0 1.0 fusion.66
  197.1 1.0 fusion.66
  198.2 1.0 fusion.66
  199.2 1.0 fusion.66
  200.3 1.0 fusion.66
  201.4 1.0 fusion.66
  202.4 1.0 fusion.66
  203.5 1.0 fusion.66
  204.6 1.0 fusion.66
  205.7 1.0 fusion.66
  206.7 1.0 fusion.66
  207.8 1.0 fusion.66
  208.9 1.0 fusion.66
  209.9 1.0 fusion.66
  211.0 1.0 fusion.66
  212.1 1.0 fusion.66
  213.2 1.0 fusion.66
  214.2 1.0 fusion.66
  215.3 1.0 fusion.66
  216.4 1.0 fusion.66
  217.4 1.0 fusion.66
  218.5 1.0 fusion.66
  219.6 1.0 fusion.66
  227.5 1.6 fusion.15
  229.1 1.0 convolution_bitcast_fusion.2
  231.8 43.3 %all-gather.11.cloned.1.call-done = bf16[256,64,128]{2,1,0:T(8,128)(2,1)} async-done(((bf16[8,64,128]{2,1,0:T(8,128)(2,1)}), bf16[256,64,128]{2,1,0:T(8,128)(2,1)}) %all-gather.11.cloned.1.call-update) | async-done | bytes 4194320 | tf_op jit(solution)/shard_map/all_gather | solution.py:13
  275.1 33.7 %while.41 = (s32[]{:T(128)}, f32[8,64,128]{2,1,0:T(8,128)S(1)}, s32[]{:T(128)}, bf16[32,8]{1,0:T(8,128)(2,1)S(1)}, bf16[32,8,64,128]{3,2,1,0:T(8,128)(2,1)}, /*index=5*/s32[]{:T(128)}, s32[]{:T(128)}) while((s32[]{:T(128)}, f32[8,64,128]{2,1,0:T(8,128)S(1)}, s32[]{:T(128)}, bf16[32,8]{1,0:T(8,128)(2,1)S(1)}, ...), condition=%wide.region_7.8_spmd.clone, body=%wide.region_6.7_spmd.clone.sunk | while | flops 327692 | bytes 655545 | solution.py:31
  308.8 1.0 convolution_bitcast_fusion.1
  309.8 1.0 fusion.21
  310.9 7.8 %fusion.2 = bf16[8192,512]{0,1:T(8,128)(2,1)} fusion(bf16[256,512]{0,1:T(8,128)(2,1)S(1)} %bitcast.107, bf16[256,8192]{1,0:T(8,128)(2,1)} %param.10), kind=kOutput, calls=%fused_computation.7 | convolution fusion | flops 2151677952 | bytes 12845056 | tf_op jit(solution)/shard_map/dot_general | solution.py:106
  319.0 7.8 %convolution_convert_fusion.1 = bf16[256,8192]{1,0:T(8,128)(2,1)} fusion(bf16[256,512]{0,1:T(8,128)(2,1)S(1)} %bitcast.108, bf16[8192,512]{1,0:T(8,128)(2,1)} %all-gather.7.cloned.1.call-done), kind=kOutput, calls=%fused_computation.8 | convolution fusion | flops 2149580800 | bytes 12845056 | tf_op jit(solution)/shard_map/dot_general | solution.py:99
  326.8 47.2 %all-reduce.3.cloned.1.call-done = (bf16[256,128]{1,0:T(8,128)(2,1)}, bf16[256,128]{1,0:T(8,128)(2,1)}) async-done(((bf16[256,128]{1,0:T(8,128)(2,1)}, bf16[256,128]{1,0:T(8,128)(2,1)}), (bf16[256,128]{1,0:T(8,128)(2,1)}, bf16[256,128]{1,0:T(8,128)(2,1)})) %all-reduce.3.cloned.1.call-update) | async-done | bytes 131088 | tf_op jit(solution)/shard_map/psum | solution.py:96
  373.9 1.5 convert_element_type.131
  375.5 1.5 convert_element_type.135
  377.0 229.8 %reduce-scatter.5.cloned.1.call-done = bf16[256,512]{0,1:T(8,128)(2,1)} async-done(((bf16[8192,512]{0,1:T(8,128)(2,1)}), bf16[256,512]{0,1:T(8,128)(2,1)}) %reduce-scatter.5.cloned.1.call-update) | async-done | bytes 262160 | tf_op jit(solution)/shard_map/reduce_scatter | solution.py:105
  606.7 1.9 copy.31
  608.6 40.7 %reduce-scatter.3.cloned.1.call-done = bf16[256,1024]{1,0:T(8,128)(2,1)} async-done(((bf16[256,8192]{1,0:T(8,128)(2,1)}), bf16[256,1024]{1,0:T(8,128)(2,1)}) %reduce-scatter.3.cloned.1.call-update) | async-done | bytes 524304 | tf_op jit(solution)/shard_map/reduce_scatter | solution.py:102
  (133 shorter events, 44.9 us)
Async XLA Ops:
  7.2 46.8 %copy-start = (bf16[256,128]{1,0:T(8,128)(2,1)S(1)}, bf16[256,128]{1,0:T(8,128)(2,1)}, u32[]{:S(2)}) copy-start(bf16[256,128]{1,0:T(8,128)(2,1)} %param.13) | copy-start | bytes 196612
  7.2 103.6 %all-gather.7.cloned.1.call-start = ((), (), s32[]{:S(2)}) async-start(), calls=%async_computation.2 | async-start | bytes 8650752 | tf_op jit(solution)/shard_map/all_gather | solution.py:50
  7.9 184.9 %all-gather.9.cloned.1.call-start = ((), (), s32[]{:S(2)}) async-start(), calls=%async_computation.5 | async-start | bytes 4325376 | tf_op jit(solution)/shard_map/all_gather | solution.py:13
  12.2 262.9 %all-gather.11.cloned.1.call-start = ((), (), s32[]{:S(2)}) async-start(), calls=%async_computation.6 | async-start | bytes 4325376 | tf_op jit(solution)/shard_map/all_gather | solution.py:13
  119.0 255.0 %all-reduce.3.cloned.1.call-start = ((), (), s32[]{:S(2)}) async-start(), calls=%async_computation.7 | async-start | bytes 262144 | tf_op jit(solution)/shard_map/psum | solution.py:96
  227.0 3.8 copy-start.1
  310.9 295.9 %reduce-scatter.5.cloned.1.call-start = ((), (), s32[]{:S(2)}) async-start(), calls=%async_computation.4 | async-start | bytes 8650752 | tf_op jit(solution)/shard_map/reduce_scatter | solution.py:105
  318.7 330.6 %reduce-scatter.3.cloned.1.call-start = ((), (), s32[]{:S(2)}) async-start(), calls=%async_computation.3 | async-start | bytes 4718592 | tf_op jit(solution)/shard_map/reduce_scatter | solution.py:102
Sparse Core Ops, SparseCore 0:
  10.6 100.1 all-gather.6
  113.9 78.8 all-gather.8
  196.0 79.0 all-gather.10
  311.0 62.9 all-reduce.2
  378.4 228.3 reduce-scatter.4
  609.7 39.6 reduce-scatter.2
where the time goes:
time: 658 us; the launch traced here: 656 us
  waiting for transfers between devices  491 us (75%)
  other arithmetic  68.8 us (10%)
  blocking collectives  41.5 us (6%)
  matrix products  34.2 us (5%)
  between operations  14.3 us (2%)
    reduce_scatter x1, waiting for transfers between devices, per_device(): lax.psum_scatter(lax.dot_general(inputs, grad_values, (((0,), (0,)), ((),...  230 us
    all_gather x2, waiting for transfers between devices, carried_in(): lax.all_gather(part.astype(kind), axis)  117 us
    select_n x64, other arithmetic, lap(): return jax.tree.map(lambda a, b: jnp.where(reached, a, b), new, before)  64.9 us
    all_gather x1, waiting for transfers between devices, per_device(): w_full = lax.all_gather(w_value, 'seq', axis=0, tiled=True)  55.8 us
    psum x1, waiting for transfers between devices, per_device(): lax.psum(grad_b.reshape(steps, states).astype(jnp.bfloat16), 'head')  47.2 us
    all_gather x1, blocking collectives, carried_in(): lax.all_gather(part.astype(kind), axis)  41.5 us
    reduce_scatter x1, waiting for transfers between devices, per_device(): lax.psum_scatter(term.astype(jnp.bfloat16), 'head', scatter_dimension=1,...  40.7 us
  transfers between devices with their start and end apart: 6, of which 6 were waited for; matrix products, arithmetic and copies ran while one was open for 11% of the time, Pallas kernels for 0%

commit v1 on v0

--- a/solution.py
+++ b/solution.py
@@ -47,7 +47,8 @@
     depth = columns // heads
     states = b_proj.shape[1]
     blocks = steps // SPAN
-    w_full = lax.all_gather(w_value, "seq", axis=0, tiled=True)
+    outgoing = jnp.stack([w_value] * lax.axis_size("seq"))
+    w_full = jnp.concatenate(lax.all_to_all(outgoing, "seq", 0, 0), axis=0)
     values = jnp.dot(inputs, w_full, preferred_element_type=jnp.float32).astype(jnp.bfloat16)
     xs = values.astype(jnp.float32).reshape(blocks, SPAN, heads, depth)
     dys = grad_out.astype(jnp.float32).reshape(blocks, SPAN, heads, depth)

time: 658 us -> 734 us (1.12)
  blocking collectives: 41.5 us -> 238 us
  waiting for transfers between devices: 491 us -> 358 us
  starting transfers between devices: 0.42 us -> 12.3 us
    all_gather x1, blocking collectives: 41.5 us -> 238 us  [carried_in(): lax.all_gather(part.astype(kind), axis)]
    all_gather x2, waiting for transfers between devices: 117 us -> 39.8 us  [carried_in(): lax.all_gather(part.astype(kind), axis)]
    all_gather x1 -> x0, waiting for transfers between devices: 55.8 us -> none  [per_device(): w_full = lax.all_gather(w_value, 'seq', axis=0, tiled=True)]
    all_to_all x0 -> x1, starting transfers between devices: none -> 11.9 us  [per_device(): w_full = jnp.concatenate(lax.all_to_all(outgoing, 'seq', 0, 0), axis=0)]
  transfers between devices with their start and end apart: 6 -> 6, of which waited for: 6 -> 4; matrix products, arithmetic and copies ran while one was open for 11% -> 9% of each run, Pallas kernels for 0% -> 0%
where the time goes in v1:
time: 734 us; the launch traced here: 733 us
  waiting for transfers between devices  358 us (49%)
  blocking collectives  238 us (32%)
  other arithmetic  68.8 us (9%)
  matrix products  31.8 us (4%)
  between operations  14 us (2%)
  starting transfers between devices  12.3 us (2%)
  local copies, waits for them, and re-layouts  7.65 us (1%)
    all_gather x1, blocking collectives, carried_in(): lax.all_gather(part.astype(kind), axis)  238 us
    reduce_scatter x1, waiting for transfers between devices, per_device(): lax.psum_scatter(lax.dot_general(inputs, grad_values, (((0,), (0,)), ((),...  230 us
    select_n x64, other arithmetic, lap(): return jax.tree.map(lambda a, b: jnp.where(reached, a, b), new, before)  65 us
    psum x1, waiting for transfers between devices, per_device(): lax.psum(grad_b.reshape(steps, states).astype(jnp.bfloat16), 'head')  47.2 us
    reduce_scatter x1, waiting for transfers between devices, per_device(): lax.psum_scatter(term.astype(jnp.bfloat16), 'head', scatter_dimension=1,...  40.8 us
    all_gather x2, waiting for transfers between devices, carried_in(): lax.all_gather(part.astype(kind), axis)  39.8 us
  transfers between devices with their start and end apart: 6, of which 4 were waited for; matrix products, arithmetic and copies ran while one was open for 9% of the time, Pallas kernels for 0%

profile of v1, /device:TPU:8, one launch (start us, length us, event | category | flops | bytes accessed | tf_op | source)
XLA Modules:
  0.0 732.6 jit_solution(6471090843430099672)
XLA Ops:
  7.2 5.2 stack.2
  12.3 11.9 %all-to-all-start = ((bf16[32,256,512]{2,1,0:T(8,128)(2,1)}), bf16[32,256,512]{2,1,0:T(8,128)(2,1)}, u32[]{:S(2)}, u32[]{:S(2)}) async-start(bf16[32,256,512]{2,1,0:T(8,128)(2,1)} %stack.2), calls=%async_computation | async-start | bytes 16777216 | tf_op jit(solution)/shard_map/all_to_all | solution.py:51
  24.9 1.1 fusion.18
  26.3 238.1 %all-gather = bf16[32,1,8]{2,1,0:T(2,128)(2,1)S(1)} all-gather(bf16[1,1,8]{2,1,0:T(2,128)(2,1)S(1)} %copy.26), channel_id=2, replica_groups=mesh['seq'=32,'head'=8] {'seq'}, dimensions={0}, use_global_device_ids=true | all-gather | bytes 528 | tf_op jit(solution)/shard_map/all_gather | solution.py:13
  264.7 7.0 convolution_convert_fusion.2
  271.8 1.1 fusion.19
  273.0 34.3 %while.40 = (s32[]{:T(128)}, f32[8,64,128]{2,1,0:T(8,128)S(1)}, s32[]{:T(128)}, bf16[32,8]{1,0:T(8,128)(2,1)S(1)}, bf16[32,8,64,128]{3,2,1,0:T(8,128)(2,1)}, /*index=5*/s32[]{:T(128)}, s32[]{:T(128)}, s32[]{:T(128)}, s32[]{:T(128)}) while((s32[]{:T(128)}, f32[8,64,128]{2,1,0:T(8,128)S(1)}, s32[]{:T(128)}, ...), condition=%wide.region_1.2_spmd.clone, body=%wide.region_0.1_spmd.clone.sunk | while | flops 327696 | bytes 655607 | solution.py:31
  273.0 1.0 fusion.66
  274.1 1.0 fusion.66
  275.2 1.0 fusion.66
  276.2 1.0 fusion.66
  277.3 1.0 fusion.66
  278.4 1.0 fusion.66
  282.7 1.0 fusion.66
  283.7 1.0 fusion.66
  284.8 1.0 fusion.66
  285.9 1.0 fusion.66
  286.9 1.0 fusion.66
  288.0 1.0 fusion.66
  289.1 1.0 fusion.66
  290.2 1.0 fusion.66
  291.2 1.0 fusion.66
  292.3 1.0 fusion.66
  293.4 1.0 fusion.66
  294.4 1.0 fusion.66
  295.5 1.0 fusion.66
  296.6 1.0 fusion.66
  297.7 1.0 fusion.66
  298.7 1.0 fusion.66
  299.8 1.0 fusion.66
  303.0 1.0 fusion.66
  304.1 1.0 fusion.66
  305.2 1.0 fusion.66
  306.2 1.0 fusion.66
  307.7 1.6 fusion.15
  309.3 1.0 convolution_bitcast_fusion.2
  312.0 39.8 %all-gather.8.cloned.1.call-done = bf16[256,64,128]{2,1,0:T(8,128)(2,1)} async-done(((bf16[8,64,128]{2,1,0:T(8,128)(2,1)}), bf16[256,64,128]{2,1,0:T(8,128)(2,1)}) %all-gather.8.cloned.1.call-update) | async-done | bytes 4194320 | tf_op jit(solution)/shard_map/all_gather | solution.py:13
  351.7 33.7 %while.41 = (s32[]{:T(128)}, f32[8,64,128]{2,1,0:T(8,128)S(1)}, s32[]{:T(128)}, bf16[32,8]{1,0:T(8,128)(2,1)S(1)}, bf16[32,8,64,128]{3,2,1,0:T(8,128)(2,1)}, /*index=5*/s32[]{:T(128)}, s32[]{:T(128)}) while((s32[]{:T(128)}, f32[8,64,128]{2,1,0:T(8,128)S(1)}, s32[]{:T(128)}, bf16[32,8]{1,0:T(8,128)(2,1)S(1)}, ...), condition=%wide.region_7.8_spmd.clone, body=%wide.region_6.7_spmd.clone.sunk | while | flops 327692 | bytes 655545 | solution.py:31
  385.4 1.0 convolution_bitcast_fusion.1
  386.5 1.0 fusion.21
  387.7 7.8 %fusion.2 = bf16[8192,512]{0,1:T(8,128)(2,1)} fusion(bf16[256,512]{0,1:T(8,128)(2,1)S(1)} %bitcast.108, bf16[256,8192]{1,0:T(8,128)(2,1)} %param.10), kind=kOutput, calls=%fused_computation.7 | convolution fusion | flops 2151677952 | bytes 12845056 | tf_op jit(solution)/shard_map/dot_general | solution.py:107
  395.6 7.8 %convolution_convert_fusion.1 = bf16[256,8192]{1,0:T(8,128)(2,1)} fusion(bf16[256,512]{0,1:T(8,128)(2,1)S(1)} %bitcast.109, bf16[8192,512]{1,0:T(8,128)(2,1)} %bitcast.19), kind=kOutput, calls=%fused_computation.8 | convolution fusion | flops 2149580800 | bytes 12845056 | tf_op jit(solution)/shard_map/dot_general | solution.py:100
  403.4 47.2 %all-reduce.3.cloned.1.call-done = (bf16[256,128]{1,0:T(8,128)(2,1)}, bf16[256,128]{1,0:T(8,128)(2,1)}) async-done(((bf16[256,128]{1,0:T(8,128)(2,1)}, bf16[256,128]{1,0:T(8,128)(2,1)}), (bf16[256,128]{1,0:T(8,128)(2,1)}, bf16[256,128]{1,0:T(8,128)(2,1)})) %all-reduce.3.cloned.1.call-update) | async-done | bytes 131088 | tf_op jit(solution)/shard_map/psum | solution.py:97
  450.6 1.5 convert_element_type.132
  452.1 1.5 convert_element_type.136
  453.6 229.8 %reduce-scatter.5.cloned.1.call-done = bf16[256,512]{0,1:T(8,128)(2,1)} async-done(((bf16[8192,512]{0,1:T(8,128)(2,1)}), bf16[256,512]{0,1:T(8,128)(2,1)}) %reduce-scatter.5.cloned.1.call-update) | async-done | bytes 262160 | tf_op jit(solution)/shard_map/reduce_scatter | solution.py:106
  683.4 1.9 copy.31
  685.2 40.8 %reduce-scatter.3.cloned.1.call-done = bf16[256,1024]{1,0:T(8,128)(2,1)} async-done(((bf16[256,8192]{1,0:T(8,128)(2,1)}), bf16[256,1024]{1,0:T(8,128)(2,1)}) %reduce-scatter.3.cloned.1.call-update) | async-done | bytes 524304 | tf_op jit(solution)/shard_map/reduce_scatter | solution.py:103
  (137 shorter events, 41.8 us)
Async XLA Ops:
  7.2 257.3 %copy-start = (bf16[256,128]{1,0:T(8,128)(2,1)S(1)}, bf16[256,128]{1,0:T(8,128)(2,1)}, u32[]{:S(2)}) copy-start(bf16[256,128]{1,0:T(8,128)(2,1)} %param.13) | copy-start | bytes 196612
  12.3 12.0 %copy-start.2 = (bf16[256,512]{1,0:T(8,128)(2,1)S(1)}, bf16[256,512]{1,0:T(8,128)(2,1)}, u32[]{:S(2)}) copy-start(bf16[256,512]{1,0:T(8,128)(2,1)} %param.15) | copy-start | bytes 786436
  12.3 12.1 %copy-start.3 = (f32[256,8]{0,1:T(8,128)S(1)}, f32[256,8]{0,1:T(8,128)}, u32[]{:S(2)}) copy-start(f32[256,8]{0,1:T(8,128)} %param.12) | copy-start | bytes 24580
  12.3 12.6 %copy-start.1 = (bf16[256,128]{1,0:T(8,128)(2,1)S(1)}, bf16[256,128]{1,0:T(8,128)(2,1)}, u32[]{:S(2)}) copy-start(bf16[256,128]{1,0:T(8,128)(2,1)} %param.14) | copy-start | bytes 196612
  12.3 252.3 %all-to-all-start = ((bf16[32,256,512]{2,1,0:T(8,128)(2,1)}), bf16[32,256,512]{2,1,0:T(8,128)(2,1)}, u32[]{:S(2)}, u32[]{:S(2)}) async-start(bf16[32,256,512]{2,1,0:T(8,128)(2,1)} %stack.2), calls=%async_computation | async-start | bytes 16777216 | tf_op jit(solution)/shard_map/all_to_all | solution.py:51
  24.2 248.7 %all-gather.6.cloned.1.call-start = ((), (), s32[]{:S(2)}) async-start(), calls=%async_computation.5 | async-start | bytes 4325376 | tf_op jit(solution)/shard_map/all_gather | solution.py:13
  26.0 325.7 %all-gather.8.cloned.1.call-start = ((), (), s32[]{:S(2)}) async-start(), calls=%async_computation.6 | async-start | bytes 4325376 | tf_op jit(solution)/shard_map/all_gather | solution.py:13
  272.9 177.7 %all-reduce.3.cloned.1.call-start = ((), (), s32[]{:S(2)}) async-start(), calls=%async_computation.7 | async-start | bytes 262144 | tf_op jit(solution)/shard_map/psum | solution.py:97
  387.5 295.8 %reduce-scatter.5.cloned.1.call-start = ((), (), s32[]{:S(2)}) async-start(), calls=%async_computation.4 | async-start | bytes 8650752 | tf_op jit(solution)/shard_map/reduce_scatter | solution.py:106
  395.6 330.5 %reduce-scatter.3.cloned.1.call-start = ((), (), s32[]{:S(2)}) async-start(), calls=%async_computation.3 | async-start | bytes 4718592 | tf_op jit(solution)/shard_map/reduce_scatter | solution.py:103
Sparse Core Ops, SparseCore 0:
  28.2 141.5 all-gather.5
  273.0 78.6 all-gather.7
  387.6 62.9 all-reduce.2
  455.0 228.3 reduce-scatter.4
  686.3 39.6 reduce-scatter.2
